TPU v7x, 32 devices: a whole 2x2x4 slice. The times are simulated.
32 devices in a mesh: rows: 4 (over y, core), cols: 8 (over z, x).
Axes of the slice: x: 2, y: 2, z: 4, core: 2. Of those that a mesh axis runs over, the one named last changes fastest.
Arguments:
- prior: float32 [64, 512, 512], P('rows', 'cols'), may hold values from -6 to 6
- obs_cell: int32 [8, 128], replicated, may hold values from 0 to 32767, as said below
- obs_weight: float32 [8, 128, 8], replicated, may hold values from 0.1 to 1
- obs_value: float32 [8, 128], replicated, may hold values from -8 to 8
- obs_var: float32 [8, 128], replicated, may hold values from 0.25 to 4
- loc_mask: int32 [8, 32], replicated, may hold values from 0 to 1, as said below
- batch_order: int32 [8], replicated, may hold values from 0 to 7, each once
- kernel: float32 [8, 7, 7], replicated, may hold values from 0.005 to 0.04
- mixing: float32 [8, 8], replicated, may hold values from -2 to 2
Outputs:
- forecast: float32 [64, 512, 512], P('rows', 'cols')
Inputs may be any that keep to these rules, and one draw needn't show every extreme that they name: `obs_cell`: all 128 cells of one batch lie in one tile, rows r * 16 to (r + 1) * 16 - 1 and columns c * 64 to (c + 1) * 64 - 1, whose index is r * 8 + c. `loc_mask`: for each batch the tiles marked 1 form a rectangle of tiles that contains the tile of that batch's cells. `batch_order`: each batch appears once.
All inputs are finite; a program needn't handle non-finite values.
Results may differ from a plain program's by a relative error of at most 0.0003.
Values sent between devices are 32-bit elements; how exact they have to be, the bound alone decides.
No kernel may reach another device: no remote copies, remote signals or barrier semaphores. Data moves between devices by JAX's collectives and lax.ppermute only.
A program may use at most 128 MiB of HBM per device.

v0:
```python
import jax
import jax.numpy as jnp
from jax import lax
from jax.sharding import PartitionSpec as P

BATCHES = 8
KW = 7
HALFW = 48


def with_halo(shard, sides, width):
    for axis, dim in sides:
        size, length = (lax.axis_size(axis), shard.shape[dim])
        up = [(i, (i + 1) % size) for i in range(size - 1)]
        down = [(j, i) for i, j in up]
        last = lax.slice_in_dim(shard, length - width, length, axis=dim)
        initial = lax.slice_in_dim(shard, 0, width, axis=dim)
        before = lax.ppermute(last, axis, up)
        after = lax.ppermute(initial, axis, down)
        shard = jnp.concatenate([before, shard, after], axis=dim)
    return shard


def taper_weights(ratio):
    clamped = jnp.maximum(ratio, 1.0)
    inner_part = (((-0.25 * ratio + 0.5) * ratio + 0.625) * ratio - 5.0 / 3.0) * ratio * ratio + 1.0
    outer_part = (
        ((((ratio / 12.0 - 0.5) * ratio + 0.625) * ratio + 5.0 / 3.0) * ratio - 5.0) * ratio
        + 4.0
        - 2.0 / (3.0 * clamped)
    )
    return jnp.where(ratio <= 1.0, inner_part, jnp.where(ratio < 2.0, outer_part, 0.0))


def batch_gain(predicted, value_row, var_row):
    mean_pred = jnp.mean(predicted, axis=1)
    spread = predicted - mean_pred[:, None]
    variance = jnp.sum(spread * spread, axis=1) / (predicted.shape[1] - 1)
    denominator = variance + var_row
    shrink = 1.0 / (1.0 + jnp.sqrt(var_row / denominator))
    kalman_gain = ((value_row - mean_pred)[:, None] - shrink[:, None] * spread) / denominator[
        :, None
    ]
    return (spread, kalman_gain)


def refresh_block(block, first_row, first_col, cell_row, cell_col, spread, kalman_gain, active):
    rows_count, cols_count, channels = block.shape
    members = spread.shape[1]
    species = channels // members
    row_pos = (first_row + jnp.arange(rows_count, dtype=jnp.int32)).astype(jnp.float32)
    col_pos = (first_col + jnp.arange(cols_count, dtype=jnp.int32)).astype(jnp.float32)
    row_gap = row_pos[:, None, None] - cell_row.astype(jnp.float32)[None, None, :]
    col_gap = col_pos[None, :, None] - cell_col.astype(jnp.float32)[None, None, :]
    squared = row_gap * row_gap + col_gap * col_gap
    taper = taper_weights(jnp.sqrt(squared) / HALFW) * active
    taper = taper.reshape(rows_count * cols_count, cell_row.shape[0])
    members_view = block.reshape(rows_count * cols_count, species, members)
    covariance = jnp.einsum(
        "psm,im->psi", members_view, spread, precision=lax.Precision.HIGHEST
    ) / (members - 1)
    increment = jnp.einsum(
        "psi,im->psm", covariance * taper[:, None, :], kalman_gain, precision=lax.Precision.HIGHEST
    )
    return (members_view + increment).reshape(rows_count, cols_count, channels)


def refresh_tile(ensemble, row_start, col_start, cell_row, cell_col, spread, kalman_gain, active):
    pieces = refresh_block(
        ensemble, row_start + 0, col_start, cell_row, cell_col, spread, kalman_gain, active
    )
    return pieces


def local_prediction(ensemble, cell_row, cell_col, weights_rows, row_start, col_start):
    tile_height, tile_width, channels = ensemble.shape
    species = weights_rows.shape[1]
    members = channels // species
    local_row = cell_row - row_start
    local_col = cell_col - col_start
    inside = (
        (local_row >= 0) & (local_row < tile_height) & (local_col >= 0) & (local_col < tile_width)
    )
    flat_index = jnp.clip(local_row, 0, tile_height - 1) * tile_width + jnp.clip(
        local_col, 0, tile_width - 1
    )
    picked = ensemble.reshape(tile_height * tile_width, species, members)[flat_index]
    predicted = jnp.einsum("is,ism->im", weights_rows, picked, precision=lax.Precision.HIGHEST)
    return jnp.where(inside[:, None], predicted, 0.0)


def shards(prior, obs_cell, obs_weight, obs_value, obs_var, loc_mask, batch_order, kernel, mixing):
    tile_height, tile_width, channels = prior.shape
    species = kernel.shape[0]
    members = channels // species
    cols_count = lax.axis_size("cols")
    grid_width = tile_width * cols_count
    row_start = lax.axis_index("rows") * tile_height
    col_start = lax.axis_index("cols") * tile_width
    my_tile = lax.axis_index("rows") * cols_count + lax.axis_index("cols")
    ensemble = prior
    for position in range(BATCHES):
        current = batch_order[position]
        obs_cells = obs_cell[current]
        cell_row = obs_cells // grid_width
        cell_col = obs_cells % grid_width
        partial_value = local_prediction(
            ensemble, cell_row, cell_col, obs_weight[current], row_start, col_start
        )
        predicted = lax.psum(partial_value, ("rows", "cols"))
        spread, kalman_gain = batch_gain(predicted, obs_value[current], obs_var[current])
        active = loc_mask[current, my_tile].astype(jnp.float32)
        ensemble = refresh_tile(
            ensemble, row_start, col_start, cell_row, cell_col, spread, kalman_gain, active
        )
    halo_width = KW // 2
    padded = with_halo(ensemble, (("rows", 0), ("cols", 1)), 3)
    padded_width = tile_width + 2 * halo_width
    offsets = (
        jnp.arange(padded_width, dtype=jnp.int32)[None, :]
        - jnp.arange(tile_width, dtype=jnp.int32)[:, None]
    )
    onehot = (offsets[:, :, None] == jnp.arange(KW, dtype=jnp.int32)[None, None, :]).astype(
        jnp.float32
    )
    band_matrix = jnp.einsum("tak,xik->taxi", kernel, onehot, precision=lax.Precision.HIGHEST)
    padded_grid = padded.reshape(tile_height + 2 * halo_width, padded_width, species, members)
    smoothed = jnp.zeros((tile_height, tile_width, species, members), jnp.float32)
    for vertical in range(KW):
        smoothed = smoothed + jnp.einsum(
            "txi,yitm->yxtm",
            band_matrix[:, vertical],
            padded_grid[vertical : vertical + tile_height],
            precision=lax.Precision.HIGHEST,
        )
    mixed_field = jnp.einsum("st,yxtm->yxsm", mixing, smoothed, precision=lax.Precision.HIGHEST)
    return mixed_field.reshape(tile_height, tile_width, channels)


def solution(mesh):
    return jax.shard_map(
        shards,
        mesh=mesh,
        in_specs=(P("rows", "cols", None), P(), P(), P(), P(), P(), P(), P(), P()),
        out_specs=P("rows", "cols", None),
        check_vma=False,
    )
```

profile of v0, /device:TPU:1, one launch (start us, length us, event | category | flops | bytes accessed | tf_op | source)
XLA Modules:
  0.0 676.1 jit_solution(12245388337613379013)
XLA Ops:
  29.4 3.6 gather_fusion
  34.7 40.8 %psum.56 = f32[128,64]{0,1:T(8,128)S(1)} all-reduce(f32[128,64]{0,1:T(8,128)S(1)} %broadcast_select_fusion.7), channel_id=1, replica_groups=mesh['rows'=4,'cols'=8] {'rows','cols'}, use_global_device_ids=true, to_apply=%region_0.1 | all-reduce | flops 8192 | bytes 65536 | tf_op jit(solution)/shard_map/psum | solution.py:110
  80.4 4.5 fusion.60
  91.1 40.8 %psum.57 = f32[128,64]{0,1:T(8,128)S(1)} all-reduce(f32[128,64]{0,1:T(8,128)S(1)} %broadcast_select_fusion.6), channel_id=1, replica_groups=mesh['rows'=4,'cols'=8] {'rows','cols'}, use_global_device_ids=true, to_apply=%region_3.4 | all-reduce | flops 8192 | bytes 65536 | tf_op jit(solution)/shard_map/psum | solution.py:110
  131.9 6.8 %fusion.242 = f32[1024,8,128]{2,0,1:T(8,128)S(1)} fusion(f32[1024,8,64]{0,2,1:T(8,128)S(1)} %fusion.60, f32[128,64]{0,1:T(8,128)S(1)} %psum.57, f32[128]{0:T(128)S(1)} %get-tuple-element.169), kind=kOutput, calls=%fused_computation.329 | convolution fusion | flops 805314560 | bytes 6324736 | tf_op jit(solution)/shard_map/psm,im->psi/dot_general | solution.py:59
  140.1 6.3 fusion.39
  146.4 4.1 copy.69
  153.8 40.1 %psum.58 = f32[128,64]{0,1:T(8,128)S(1)} all-reduce(f32[128,64]{0,1:T(8,128)S(1)} %broadcast_select_fusion.5), channel_id=1, replica_groups=mesh['rows'=4,'cols'=8] {'rows','cols'}, use_global_device_ids=true, to_apply=%region_6.7 | all-reduce | flops 8192 | bytes 65536 | tf_op jit(solution)/shard_map/psum | solution.py:110
  194.1 6.8 %fusion.239 = f32[1024,8,128]{2,0,1:T(8,128)S(1)} fusion(f32[1024,8,64]{0,2,1:T(8,128)S(1)} %copy-done.2, f32[128,64]{0,1:T(8,128)S(1)} %psum.58, f32[128]{0:T(128)S(1)} %get-tuple-element.167), kind=kOutput, calls=%fused_computation.326 | convolution fusion | flops 805314560 | bytes 6324736 | tf_op jit(solution)/shard_map/psm,im->psi/dot_general | solution.py:59
  202.3 6.3 fusion.42
  208.6 4.4 copy.70
  216.3 40.2 %psum.59 = f32[128,64]{0,1:T(8,128)S(1)} all-reduce(f32[128,64]{0,1:T(8,128)S(1)} %broadcast_select_fusion.4), channel_id=1, replica_groups=mesh['rows'=4,'cols'=8] {'rows','cols'}, use_global_device_ids=true, to_apply=%region_9.10 | all-reduce | flops 8192 | bytes 65536 | tf_op jit(solution)/shard_map/psum | solution.py:110
  256.6 6.8 %fusion.236 = f32[1024,8,128]{2,0,1:T(8,128)S(1)} fusion(f32[1024,8,64]{0,2,1:T(8,128)S(1)} %copy-done.3, f32[128,64]{0,1:T(8,128)S(1)} %psum.59, f32[128]{0:T(128)S(1)} %get-tuple-element.165), kind=kOutput, calls=%fused_computation.323 | convolution fusion | flops 805314560 | bytes 6324736 | tf_op jit(solution)/shard_map/psm,im->psi/dot_general | solution.py:59
  264.8 6.3 fusion.45
  271.1 4.1 copy.71
  278.6 40.1 %psum.60 = f32[128,64]{0,1:T(8,128)S(1)} all-reduce(f32[128,64]{0,1:T(8,128)S(1)} %broadcast_select_fusion.3), channel_id=1, replica_groups=mesh['rows'=4,'cols'=8] {'rows','cols'}, use_global_device_ids=true, to_apply=%region_12.13 | all-reduce | flops 8192 | bytes 65536 | tf_op jit(solution)/shard_map/psum | solution.py:110
  318.8 6.8 %fusion.233 = f32[1024,8,128]{2,0,1:T(8,128)S(1)} fusion(f32[1024,8,64]{0,2,1:T(8,128)S(1)} %copy-done.4, f32[128,64]{0,1:T(8,128)S(1)} %psum.60, f32[128]{0:T(128)S(1)} %get-tuple-element.163), kind=kOutput, calls=%fused_computation.320 | convolution fusion | flops 805314560 | bytes 6324736 | tf_op jit(solution)/shard_map/psm,im->psi/dot_general | solution.py:59
  327.0 6.3 fusion.48
  333.3 4.4 copy.72
  341.0 40.2 %psum.61 = f32[128,64]{0,1:T(8,128)S(1)} all-reduce(f32[128,64]{0,1:T(8,128)S(1)} %broadcast_select_fusion.2), channel_id=1, replica_groups=mesh['rows'=4,'cols'=8] {'rows','cols'}, use_global_device_ids=true, to_apply=%region_15.16 | all-reduce | flops 8192 | bytes 65536 | tf_op jit(solution)/shard_map/psum | solution.py:110
  381.4 6.8 %fusion.230 = f32[1024,8,128]{2,0,1:T(8,128)S(1)} fusion(f32[1024,8,64]{0,2,1:T(8,128)S(1)} %copy-done.5, f32[128,64]{0,1:T(8,128)S(1)} %psum.61, f32[128]{0:T(128)S(1)} %get-tuple-element.161), kind=kOutput, calls=%fused_computation.317 | convolution fusion | flops 805314560 | bytes 6324736 | tf_op jit(solution)/shard_map/psm,im->psi/dot_general | solution.py:59
  389.6 6.3 fusion.51
  395.9 4.0 copy.73
  403.2 40.3 %psum.62 = f32[128,64]{0,1:T(8,128)S(1)} all-reduce(f32[128,64]{0,1:T(8,128)S(1)} %broadcast_select_fusion.1), channel_id=1, replica_groups=mesh['rows'=4,'cols'=8] {'rows','cols'}, use_global_device_ids=true, to_apply=%region_18.19 | all-reduce | flops 8192 | bytes 65536 | tf_op jit(solution)/shard_map/psum | solution.py:110
  443.5 6.8 %fusion.227 = f32[1024,8,128]{2,0,1:T(8,128)S(1)} fusion(f32[1024,8,64]{0,2,1:T(8,128)S(1)} %copy-done.6, f32[128,64]{0,1:T(8,128)S(1)} %psum.62, f32[128]{0:T(128)S(1)} %get-tuple-element.159), kind=kOutput, calls=%fused_computation.314 | convolution fusion | flops 805314560 | bytes 6324736 | tf_op jit(solution)/shard_map/psm,im->psi/dot_general | solution.py:59
  451.6 4.9 fusion.54
  462.7 40.7 %psum.63 = f32[128,64]{0,1:T(8,128)S(1)} all-reduce(f32[128,64]{0,1:T(8,128)S(1)} %broadcast_select_fusion), channel_id=1, replica_groups=mesh['rows'=4,'cols'=8] {'rows','cols'}, use_global_device_ids=true, to_apply=%region_21.22 | all-reduce | flops 8192 | bytes 65536 | tf_op jit(solution)/shard_map/psum | solution.py:110
  503.5 6.8 %fusion.224 = f32[1024,8,128]{2,0,1:T(8,128)S(1)} fusion(f32[1024,8,64]{0,2,1:T(8,128)S(1)} %fusion.54, f32[128,64]{0,1:T(8,128)S(1)} %psum.63, f32[128]{0:T(128)S(1)} %get-tuple-element.133), kind=kOutput, calls=%fused_computation.311 | convolution fusion | flops 805314560 | bytes 6324736 | tf_op jit(solution)/shard_map/psm,im->psi/dot_general | solution.py:59
  511.6 4.9 fusion.57
  521.4 5.4 collective-permute-start
  542.9 3.9 collective-permute-done.2
  548.4 5.2 fusion.409
  553.6 4.6 reshape.2901
  558.2 4.6 reshape.2900
  562.8 4.6 reshape.2905
  567.4 4.6 reshape.2904
  572.0 4.6 reshape.2903
  576.7 4.6 reshape.2902
  583.9 10.3 %fusion.10 = f32[8,16,64,64]{3,2,1,0:T(8,128)S(1)} fusion(f32[16,70,8,64]{3,2,1,0:T(8,128)} %reshape.2901, f32[8,64,70,1]{2,0,1,3:T(8,128)} %get-tuple-element.61), kind=kOutput, calls=%fused_computation.18 | convolution fusion | flops 440401920 | bytes 4534272 | tf_op jit(solution)/shard_map/txi,yitm->yxtm/dot_general | solution.py:130
  594.2 11.8 %fusion.12 = f32[8,16,64,64]{3,2,1,0:T(8,128)} fusion(f32[16,70,8,64]{3,2,1,0:T(8,128)} %reshape.2900, f32[8,64,70,1]{2,0,1,3:T(8,128)S(1)} %copy-done.17), kind=kOutput, calls=%fused_computation.20 | convolution fusion | flops 440401920 | bytes 4534272 | tf_op jit(solution)/shard_map/txi,yitm->yxtm/dot_general | solution.py:130
  606.1 9.4 %fusion.2 = f32[8,16,64,64]{3,2,1,0:T(8,128)} fusion(f32[16,70,8,64]{3,2,1,0:T(8,128)S(1)} %bitcast.856, f32[8,64,70,1]{2,0,1,3:T(8,128)S(1)} %copy-done.16), kind=kOutput, calls=%fused_computation.10 | convolution fusion | flops 440401920 | bytes 4534272 | tf_op jit(solution)/shard_map/txi,yitm->yxtm/dot_general | solution.py:130
  615.5 9.9 %fusion.4 = f32[8,16,64,64]{3,2,1,0:T(8,128)} fusion(f32[16,70,8,64]{3,2,1,0:T(8,128)S(1)} %bitcast.854, f32[8,64,70,1]{2,0,1,3:T(8,128)S(1)} %copy-done.15), kind=kOutput, calls=%fused_computation.12 | convolution fusion | flops 440401920 | bytes 4534272 | tf_op jit(solution)/shard_map/txi,yitm->yxtm/dot_general | solution.py:130
  625.4 9.5 %fusion.6 = f32[8,16,64,64]{3,2,1,0:T(8,128)} fusion(f32[16,70,8,64]{3,2,1,0:T(8,128)S(1)} %bitcast.852, f32[8,64,70,1]{2,0,1,3:T(8,128)S(1)} %copy-done.14), kind=kOutput, calls=%fused_computation.14 | convolution fusion | flops 440401920 | bytes 4534272 | tf_op jit(solution)/shard_map/txi,yitm->yxtm/dot_general | solution.py:130
  635.0 9.4 %fusion.8 = f32[8,16,64,64]{3,2,1,0:T(8,128)} fusion(f32[16,70,8,64]{3,2,1,0:T(8,128)S(1)} %bitcast.850, f32[8,64,70,1]{2,0,1,3:T(8,128)S(1)} %get-tuple-element.60), kind=kOutput, calls=%fused_computation.16 | convolution fusion | flops 440401920 | bytes 4534272 | tf_op jit(solution)/shard_map/txi,yitm->yxtm/dot_general | solution.py:130
  644.4 13.5 %add_bitcast_fusion = f32[16,64,8,64]{1,3,0,2:T(8,128)} fusion(f32[8,16,64,64]{3,2,1,0:T(8,128)S(1)} %copy-done.10, f32[8,16,64,64]{3,2,1,0:T(8,128)} %fusion.4, f32[8,16,64,64]{3,2,1,0:T(8,128)} %fusion.6, f32[8,16,64,64]{3,2,1,0:T(8,128)} %fusion.8, f32[8,16,64,64]{3,2,1,0:T(8,128)S(1)} %copy-done.9, f32[8,16,64,64]{3,2,1,0:T(8,128)S(1)} %fusion.10, ...), kind=kOutput, calls=%fused_computation.24 | convolution fusion | flops 443547648 | bytes 17117184 | tf_op jit(solution)/shard_map/txi,yitm->yxtm/dot_general | solution.py:130
  657.9 5.3 copy.99
  663.3 7.8 %convolution_bitcast_fusion = f32[16,64,8,64]{3,2,1,0:T(8,128)} fusion(f32[16,64,8,64]{3,2,1,0:T(8,128)} %copy.99, f32[8,8]{1,0:T(8,128)S(1)} %copy-done.45), kind=kOutput, calls=%fused_computation.40 | convolution fusion | flops 50331648 | bytes 4194560 | tf_op jit(solution)/shard_map/st,yxtm->yxsm/dot_general | solution.py:136
  671.1 4.8 reshape.2792
  (290 shorter events, 79.5 us)
Async XLA Ops:
  0.0 534.7 %copy-start = (f32[8,7,7]{2,0,1:T(8,128)S(1)}, f32[8,7,7]{2,0,1:T(8,128)}, u32[]{:S(2)}) copy-start(f32[8,7,7]{2,0,1:T(8,128)} %param.16) | copy-start | bytes 4708
  0.0 24.1 %copy-start.13 = (f32[16,64,512]{2,1,0:T(8,128)S(1)}, f32[16,64,512]{2,1,0:T(8,128)}, u32[]{:S(2)}) copy-start(f32[16,64,512]{2,1,0:T(8,128)} %param.9) | copy-start | bytes 6291460
  29.4 50.4 %copy-start.8 = (f32[1024,8,64]{0,2,1:T(8,128)}, f32[1024,8,64]{0,2,1:T(8,128)S(1)}, u32[]{:S(2)}) copy-start(f32[1024,8,64]{0,2,1:T(8,128)S(1)} %copy.67) | copy-start | bytes 6291460
  85.0 46.9 %copy-start.46 = (f32[8,128]{1,0:T(8,128)S(1)}, f32[8,128]{1,0:T(8,128)}, u32[]{:S(2)}) copy-start(f32[8,128]{1,0:T(8,128)} %param.12) | copy-start | bytes 12292
  87.7 51.0 %copy-start.47 = (f32[8,128]{1,0:T(8,128)S(1)}, f32[8,128]{1,0:T(8,128)}, u32[]{:S(2)}) copy-start(f32[8,128]{1,0:T(8,128)} %param.13) | copy-start | bytes 12292
  87.8 51.6 %copy-start.22 = (f32[16,128]{1,0:T(8,128)S(1)}, f32[16,128]{1,0:T(8,128)}, u32[]{:S(2)}) copy-start(f32[16,128]{1,0:T(8,128)} %get-tuple-element.135) | copy-start | bytes 24580
  146.3 7.4 %copy-start.41 = (s32[128]{0:T(128)S(1)}, s32[128]{0:T(128)}, u32[]{:S(2)}) copy-start(s32[128]{0:T(128)} %copy-done.40) | copy-start | bytes 1540
  146.3 7.5 %copy-start.53 = (s32[128]{0:T(128)S(1)}, s32[128]{0:T(128)}, u32[]{:S(2)}) copy-start(s32[128]{0:T(128)} %get-tuple-element.107) | copy-start | bytes 1540
  146.4 47.7 %copy-start.2 = (f32[1024,8,64]{0,2,1:T(8,128)S(1)}, f32[1024,8,64]{0,2,1:T(8,128)}, u32[]{:S(2)}) copy-start(f32[1024,8,64]{0,2,1:T(8,128)} %fusion.39) | copy-start | bytes 6291460
  150.5 51.0 %copy-start.21 = (f32[16,128]{1,0:T(8,128)S(1)}, f32[16,128]{1,0:T(8,128)}, u32[]{:S(2)}) copy-start(f32[16,128]{1,0:T(8,128)} %get-tuple-element.136) | copy-start | bytes 24580
  208.6 7.7 %copy-start.39 = (s32[128]{0:T(128)S(1)}, s32[128]{0:T(128)}, u32[]{:S(2)}) copy-start(s32[128]{0:T(128)} %copy-done.38) | copy-start | bytes 1540
  208.6 7.7 %copy-start.52 = (s32[128]{0:T(128)S(1)}, s32[128]{0:T(128)}, u32[]{:S(2)}) copy-start(s32[128]{0:T(128)} %get-tuple-element.104) | copy-start | bytes 1540
  208.6 48.0 %copy-start.3 = (f32[1024,8,64]{0,2,1:T(8,128)S(1)}, f32[1024,8,64]{0,2,1:T(8,128)}, u32[]{:S(2)}) copy-start(f32[1024,8,64]{0,2,1:T(8,128)} %fusion.42) | copy-start | bytes 6291460
  213.0 51.1 %copy-start.20 = (f32[16,128]{1,0:T(8,128)S(1)}, f32[16,128]{1,0:T(8,128)}, u32[]{:S(2)}) copy-start(f32[16,128]{1,0:T(8,128)} %get-tuple-element.137) | copy-start | bytes 24580
  271.1 7.4 %copy-start.37 = (s32[128]{0:T(128)S(1)}, s32[128]{0:T(128)}, u32[]{:S(2)}) copy-start(s32[128]{0:T(128)} %copy-done.36) | copy-start | bytes 1540
  271.1 7.5 %copy-start.51 = (s32[128]{0:T(128)S(1)}, s32[128]{0:T(128)}, u32[]{:S(2)}) copy-start(s32[128]{0:T(128)} %get-tuple-element.122) | copy-start | bytes 1540
  271.1 47.7 %copy-start.4 = (f32[1024,8,64]{0,2,1:T(8,128)S(1)}, f32[1024,8,64]{0,2,1:T(8,128)}, u32[]{:S(2)}) copy-start(f32[1024,8,64]{0,2,1:T(8,128)} %fusion.45) | copy-start | bytes 6291460
  275.3 51.0 %copy-start.19 = (f32[16,128]{1,0:T(8,128)S(1)}, f32[16,128]{1,0:T(8,128)}, u32[]{:S(2)}) copy-start(f32[16,128]{1,0:T(8,128)} %get-tuple-element.138) | copy-start | bytes 24580
  333.3 7.7 %copy-start.35 = (s32[128]{0:T(128)S(1)}, s32[128]{0:T(128)}, u32[]{:S(2)}) copy-start(s32[128]{0:T(128)} %copy-done.34) | copy-start | bytes 1540
  333.3 7.7 %copy-start.50 = (s32[128]{0:T(128)S(1)}, s32[128]{0:T(128)}, u32[]{:S(2)}) copy-start(s32[128]{0:T(128)} %get-tuple-element.119) | copy-start | bytes 1540
  333.3 48.0 %copy-start.5 = (f32[1024,8,64]{0,2,1:T(8,128)S(1)}, f32[1024,8,64]{0,2,1:T(8,128)}, u32[]{:S(2)}) copy-start(f32[1024,8,64]{0,2,1:T(8,128)} %fusion.48) | copy-start | bytes 6291460
  337.7 51.1 %copy-start.18 = (f32[16,128]{1,0:T(8,128)S(1)}, f32[16,128]{1,0:T(8,128)}, u32[]{:S(2)}) copy-start(f32[16,128]{1,0:T(8,128)} %get-tuple-element.139) | copy-start | bytes 24580
  395.8 7.3 %copy-start.33 = (s32[128]{0:T(128)S(1)}, s32[128]{0:T(128)}, u32[]{:S(2)}) copy-start(s32[128]{0:T(128)} %copy-done.32) | copy-start | bytes 1540
  395.8 7.3 %copy-start.49 = (s32[128]{0:T(128)S(1)}, s32[128]{0:T(128)}, u32[]{:S(2)}) copy-start(s32[128]{0:T(128)} %get-tuple-element.116) | copy-start | bytes 1540
  395.8 47.6 %copy-start.6 = (f32[1024,8,64]{0,2,1:T(8,128)S(1)}, f32[1024,8,64]{0,2,1:T(8,128)}, u32[]{:S(2)}) copy-start(f32[1024,8,64]{0,2,1:T(8,128)} %fusion.51) | copy-start | bytes 6291460
  443.5 8.1 %copy-start.7 = (f32[1024,8,64]{0,2,1:T(8,128)S(1)}, f32[1024,8,64]{0,2,1:T(8,128)}, u32[]{:S(2)}) copy-start(f32[1024,8,64]{0,2,1:T(8,128)} %fusion.51) | copy-start | bytes 6291460
  518.9 10.3 %copy-start.12 = (f32[1024,8,64]{0,2,1:T(8,128)S(1)}, f32[1024,8,64]{0,2,1:T(8,128)}, u32[]{:S(2)}) copy-start(f32[1024,8,64]{0,2,1:T(8,128)} %copy-done.11) | copy-start | bytes 6291460
  521.4 14.1 %collective-permute-start = (f32[3,64,512]{2,1,0:T(8,128)}, f32[3,64,512]{2,1,0:T(8,128)}, u32[]{:S(2)}, u32[]{:S(2)}) collective-permute-start(f32[3,64,512]{2,1,0:T(8,128)} %slice.114), channel_id=1, source_target_pairs={{0,8},{8,16},{16,24},{1,9},{9,17},{17,25},{2,10},{10,18},{18,26},{... | collective-permute-start | bytes 1179656 | tf_op jit(solution)/shard_map/ppermute | solution.py:18
  527.4 9.1 %collective-permute-start.1 = (f32[3,64,512]{2,1,0:T(8,128)S(1)}, f32[3,64,512]{2,1,0:T(8,128)S(1)}, u32[]{:S(2)}, u32[]{:S(2)}) collective-permute-start(f32[3,64,512]{2,1,0:T(8,128)S(1)} %slice.116), channel_id=1, source_target_pairs={{8,0},{16,8},{24,16},{9,1},{17,9},{25,17},{10,2},{18,10},{26,18},{... | collective-permute-start | bytes 1179656 | tf_op jit(solution)/shard_map/ppermute | solution.py:19
  537.4 9.4 %collective-permute-start.2 = (f32[22,3,512]{2,1,0:T(4,128)S(1)}, f32[22,3,512]{2,1,0:T(4,128)S(1)}, u32[]{:S(2)}, u32[]{:S(2)}) collective-permute-start(f32[22,3,512]{2,1,0:T(4,128)S(1)} %get-tuple-element.52), channel_id=1, source_target_pairs={{0,1},{1,2},{2,3},{3,4},{4,5},{5,6},{6,7},{8,9},{9,10},{10,11},{11... | collective-permute-start | bytes 405512 | tf_op jit(solution)/shard_map/ppermute | solution.py:18
  540.5 6.4 collective-permute-start.3
  581.3 24.8 %slice-start.6 = ((s8[4587520]{0:T(1024)(128)(4,1)}), s8[393216]{0:T(1024)(128)(4,1)S(1)}, s32[]{:S(2)}) async-start(s8[4587520]{0:T(1024)(128)(4,1)} %bitcast.855), calls=%async_computation.6 | async-start | bytes 786432
  583.9 10.3 %copy-start.17 = (f32[8,64,70,1]{2,0,1,3:T(8,128)S(1)}, f32[8,64,70,1]{2,0,1,3:T(8,128)}, u32[]{:S(2)}) copy-start(f32[8,64,70,1]{2,0,1,3:T(8,128)} %get-tuple-element.62) | copy-start | bytes 430084
  583.9 22.2 %slice-start.7 = ((s8[4587520]{0:T(1024)(128)(4,1)}), s8[4194304]{0:T(1024)(128)(4,1)S(1)}, s32[]{:S(2)}) async-start(s8[4587520]{0:T(1024)(128)(4,1)} %bitcast.855), calls=%async_computation.7 | async-start | bytes 8388608
  594.2 11.8 %copy-start.16 = (f32[8,64,70,1]{2,0,1,3:T(8,128)S(1)}, f32[8,64,70,1]{2,0,1,3:T(8,128)}, u32[]{:S(2)}) copy-start(f32[8,64,70,1]{2,0,1,3:T(8,128)} %get-tuple-element.57) | copy-start | bytes 430084
  594.2 21.3 %slice-start.4 = ((s8[4587520]{0:T(1024)(128)(4,1)}), s8[4194304]{0:T(1024)(128)(4,1)S(1)}, s32[]{:S(2)}) async-start(s8[4587520]{0:T(1024)(128)(4,1)} %bitcast.853), calls=%async_computation.4 | async-start | bytes 8388608
  594.2 31.2 %slice-start.2 = ((s8[4587520]{0:T(1024)(128)(4,1)}), s8[4194304]{0:T(1024)(128)(4,1)S(1)}, s32[]{:S(2)}) async-start(s8[4587520]{0:T(1024)(128)(4,1)} %bitcast.851), calls=%async_computation.2 | async-start | bytes 8388608
  606.1 9.4 %slice-start.5 = ((s8[4587520]{0:T(1024)(128)(4,1)}), s8[393216]{0:T(1024)(128)(4,1)S(1)}, s32[]{:S(2)}) async-start(s8[4587520]{0:T(1024)(128)(4,1)} %bitcast.853), calls=%async_computation.5 | async-start | bytes 786432
  606.1 9.4 %copy-start.15 = (f32[8,64,70,1]{2,0,1,3:T(8,128)S(1)}, f32[8,64,70,1]{2,0,1,3:T(8,128)}, u32[]{:S(2)}) copy-start(f32[8,64,70,1]{2,0,1,3:T(8,128)} %get-tuple-element.58) | copy-start | bytes 430084
  606.1 19.3 %slice-start.3 = ((s8[4587520]{0:T(1024)(128)(4,1)}), s8[393216]{0:T(1024)(128)(4,1)S(1)}, s32[]{:S(2)}) async-start(s8[4587520]{0:T(1024)(128)(4,1)} %bitcast.851), calls=%async_computation.3 | async-start | bytes 786432
  615.5 9.9 %copy-start.14 = (f32[8,64,70,1]{2,0,1,3:T(8,128)S(1)}, f32[8,64,70,1]{2,0,1,3:T(8,128)}, u32[]{:S(2)}) copy-start(f32[8,64,70,1]{2,0,1,3:T(8,128)} %get-tuple-element.59) | copy-start | bytes 430084
  615.5 19.4 %slice-start = ((s8[4587520]{0:T(1024)(128)(4,1)}), s8[4194304]{0:T(1024)(128)(4,1)S(1)}, s32[]{:S(2)}) async-start(s8[4587520]{0:T(1024)(128)(4,1)} %bitcast.849), calls=%async_computation | async-start | bytes 8388608
  625.4 9.6 %slice-start.1 = ((s8[4587520]{0:T(1024)(128)(4,1)}), s8[393216]{0:T(1024)(128)(4,1)S(1)}, s32[]{:S(2)}) async-start(s8[4587520]{0:T(1024)(128)(4,1)} %bitcast.849), calls=%async_computation.1 | async-start | bytes 786432
  625.4 19.0 %slice-start.8 = ((s8[4587520]{0:T(1024)(128)(4,1)}), s8[4194304]{0:T(1024)(128)(4,1)S(1)}, s32[]{:S(2)}) async-start(s8[4587520]{0:T(1024)(128)(4,1)} %bitcast.857), calls=%async_computation.8 | async-start | bytes 8388608
  635.0 9.4 %slice-start.9 = ((s8[4587520]{0:T(1024)(128)(4,1)}), s8[393216]{0:T(1024)(128)(4,1)S(1)}, s32[]{:S(2)}) async-start(s8[4587520]{0:T(1024)(128)(4,1)} %bitcast.857), calls=%async_computation.9 | async-start | bytes 786432
  635.0 9.4 %copy-start.9 = (f32[8,16,64,64]{3,2,1,0:T(8,128)S(1)}, f32[8,16,64,64]{3,2,1,0:T(8,128)}, u32[]{:S(2)}) copy-start(f32[8,16,64,64]{3,2,1,0:T(8,128)} %fusion.12) | copy-start | bytes 6291460
  635.0 9.4 %copy-start.10 = (f32[8,16,64,64]{3,2,1,0:T(8,128)S(1)}, f32[8,16,64,64]{3,2,1,0:T(8,128)}, u32[]{:S(2)}) copy-start(f32[8,16,64,64]{3,2,1,0:T(8,128)} %fusion.2) | copy-start | bytes 6291460
  663.3 12.6 %copy-start.1 = (f32[8,7,7]{2,0,1:T(8,128)S(1)}, f32[8,7,7]{2,0,1:T(8,128)}, u32[]{:S(2)}) copy-start(f32[8,7,7]{2,0,1:T(8,128)} %param.16) | copy-start | bytes 4708
  (28 other events, 120.7 us)
where the time goes:
time: 687 us; the launch traced here: 676 us
  blocking collectives  323 us (47%)
  matrix products  179 us (26%)
  local copies, waits for them, and re-layouts  118 us (17%)
  between operations  21.8 us (3%)
  other arithmetic  17 us (2%)
  starting transfers between devices  11.7 us (2%)
    psum x8, blocking collectives, shards(): predicted = lax.psum(partial_value, ('rows', 'cols'))  323 us
    dot_general x7, matrix products, shards(): jnp.einsum('txi,yitm->yxtm', band_matrix[:, vertical], padded_grid[vertic...  73.8 us
    dot_general x8, matrix products, refresh_block(): jnp.einsum('psm,im->psi', members_view, spread, precision=lax.Precision.H...  50.9 us
    dot_general x8, matrix products, refresh_block(): jnp.einsum('psi,im->psm', covariance * taper[:, None, :], kalman_gain, pr...  45.7 us
    slice x8, local copies, waits for them, and re-layouts, shards(): padded_grid[vertical:vertical + tile_height]  35.5 us
    add x7, local copies, waits for them, and re-layouts, refresh_block(): return (members_view + increment).reshape(rows_count, cols_count, channels)  26.4 us
    gather x8, local copies, waits for them, and re-layouts, local_prediction(): ensemble.reshape(tile_height * tile_width, species, members)[flat_index]  23.4 us
  transfers between devices with their start and end apart: 4, of which 3 were waited for; matrix products, arithmetic and copies ran while one was open for 1% of the time, Pallas kernels for 0%

commit v1 on v0

--- a/solution.py
+++ b/solution.py
@@ -107,7 +107,9 @@
         partial_value = local_prediction(
             ensemble, cell_row, cell_col, obs_weight[current], row_start, col_start
         )
-        predicted = lax.psum(partial_value, ("rows", "cols"))
+        predicted = partial_value
+        for over in ("cols", "rows"):
+            predicted = lax.psum(predicted, over)
         spread, kalman_gain = batch_gain(predicted, obs_value[current], obs_var[current])
         active = loc_mask[current, my_tile].astype(jnp.float32)
         ensemble = refresh_tile(

time: 687 us -> 712 us (1.036)
  blocking collectives: 323 us -> 352 us
    psum x8 -> x16, blocking collectives: 323 us -> 352 us  [shards(): predicted = lax.psum(predicted, over)]
where the time goes in v1:
time: 712 us; the launch traced here: 702 us
  blocking collectives  352 us (49%)
  matrix products  179 us (25%)
  local copies, waits for them, and re-layouts  119 us (17%)
  between operations  21.8 us (3%)
  other arithmetic  17 us (2%)
  starting transfers between devices  8.28 us (1%)
    psum x16, blocking collectives, shards(): predicted = lax.psum(predicted, over)  352 us
    dot_general x7, matrix products, shards(): jnp.einsum('txi,yitm->yxtm', band_matrix[:, vertical], padded_grid[vertic...  73.8 us
    dot_general x8, matrix products, refresh_block(): jnp.einsum('psm,im->psi', members_view, spread, precision=lax.Precision.H...  50.9 us
    dot_general x8, matrix products, refresh_block(): jnp.einsum('psi,im->psm', covariance * taper[:, None, :], kalman_gain, pr...  45.7 us
    slice x8, local copies, waits for them, and re-layouts, shards(): padded_grid[vertical:vertical + tile_height]  35.4 us
    add x7, local copies, waits for them, and re-layouts, refresh_block(): return (members_view + increment).reshape(rows_count, cols_count, channels)  27.1 us
    gather x8, local copies, waits for them, and re-layouts, local_prediction(): ensemble.reshape(tile_height * tile_width, species, members)[flat_index]  23.5 us
  transfers between devices with their start and end apart: 4, of which 3 were waited for; matrix products, arithmetic and copies ran while one was open for 1% of the time, Pallas kernels for 0%

profile of v1, /device:TPU:1, one launch (start us, length us, event | category | flops | bytes accessed | tf_op | source)
XLA Modules:
  0.0 702.3 jit_solution(4542431917750629813)
XLA Ops:
  34.9 31.1 %psum.112 = f32[128,64]{0,1:T(8,128)S(1)} all-reduce(f32[128,64]{0,1:T(8,128)S(1)} %broadcast_select_fusion.7), channel_id=1, replica_groups=mesh['rows'=4,'cols'=8] {'cols'}, use_global_device_ids=true, to_apply=%region_0.1 | all-reduce | flops 8192 | bytes 65536 | tf_op jit(solution)/shard_map/psum | solution.py:112
  66.0 17.7 %psum.113 = f32[128,64]{0,1:T(8,128)S(1)} all-reduce(f32[128,64]{0,1:T(8,128)S(1)} %psum.112), channel_id=1, replica_groups=mesh['rows'=4,'cols'=8] {'rows'}, use_global_device_ids=true, to_apply=%region_1.2 | all-reduce | flops 8192 | bytes 65536 | tf_op jit(solution)/shard_map/psum | solution.py:112
  88.6 4.5 fusion.60
  99.2 26.1 %psum.114 = f32[128,64]{0,1:T(8,128)S(1)} all-reduce(f32[128,64]{0,1:T(8,128)S(1)} %broadcast_select_fusion.6), channel_id=1, replica_groups=mesh['rows'=4,'cols'=8] {'cols'}, use_global_device_ids=true, to_apply=%region_4.5 | all-reduce | flops 8192 | bytes 65536 | tf_op jit(solution)/shard_map/psum | solution.py:112
  125.3 17.4 %psum.115 = f32[128,64]{0,1:T(8,128)S(1)} all-reduce(f32[128,64]{0,1:T(8,128)S(1)} %psum.114), channel_id=1, replica_groups=mesh['rows'=4,'cols'=8] {'rows'}, use_global_device_ids=true, to_apply=%region_5.6 | all-reduce | flops 8192 | bytes 65536 | tf_op jit(solution)/shard_map/psum | solution.py:112
  142.7 6.8 fusion.242
  151.0 6.3 fusion.39
  165.0 26.1 %psum.116 = f32[128,64]{0,1:T(8,128)S(1)} all-reduce(f32[128,64]{0,1:T(8,128)S(1)} %broadcast_select_fusion.5), channel_id=1, replica_groups=mesh['rows'=4,'cols'=8] {'cols'}, use_global_device_ids=true, to_apply=%region_8.9 | all-reduce | flops 8192 | bytes 65536 | tf_op jit(solution)/shard_map/psum | solution.py:112
  191.1 17.2 %psum.117 = f32[128,64]{0,1:T(8,128)S(1)} all-reduce(f32[128,64]{0,1:T(8,128)S(1)} %psum.116), channel_id=1, replica_groups=mesh['rows'=4,'cols'=8] {'rows'}, use_global_device_ids=true, to_apply=%region_9.10 | all-reduce | flops 8192 | bytes 65536 | tf_op jit(solution)/shard_map/psum | solution.py:112
  208.4 6.8 fusion.239
  216.5 6.3 fusion.42
  230.2 26.1 %psum.118 = f32[128,64]{0,1:T(8,128)S(1)} all-reduce(f32[128,64]{0,1:T(8,128)S(1)} %broadcast_select_fusion.4), channel_id=1, replica_groups=mesh['rows'=4,'cols'=8] {'cols'}, use_global_device_ids=true, to_apply=%region_12.13 | all-reduce | flops 8192 | bytes 65536 | tf_op jit(solution)/shard_map/psum | solution.py:112
  256.3 17.2 %psum.119 = f32[128,64]{0,1:T(8,128)S(1)} all-reduce(f32[128,64]{0,1:T(8,128)S(1)} %psum.118), channel_id=1, replica_groups=mesh['rows'=4,'cols'=8] {'rows'}, use_global_device_ids=true, to_apply=%region_13.14 | all-reduce | flops 8192 | bytes 65536 | tf_op jit(solution)/shard_map/psum | solution.py:112
  273.6 6.8 fusion.236
  281.8 6.3 fusion.45
  295.9 26.1 %psum.120 = f32[128,64]{0,1:T(8,128)S(1)} all-reduce(f32[128,64]{0,1:T(8,128)S(1)} %broadcast_select_fusion.3), channel_id=1, replica_groups=mesh['rows'=4,'cols'=8] {'cols'}, use_global_device_ids=true, to_apply=%region_16.17 | all-reduce | flops 8192 | bytes 65536 | tf_op jit(solution)/shard_map/psum | solution.py:112
  322.0 17.2 %psum.121 = f32[128,64]{0,1:T(8,128)S(1)} all-reduce(f32[128,64]{0,1:T(8,128)S(1)} %psum.120), channel_id=1, replica_groups=mesh['rows'=4,'cols'=8] {'rows'}, use_global_device_ids=true, to_apply=%region_17.18 | all-reduce | flops 8192 | bytes 65536 | tf_op jit(solution)/shard_map/psum | solution.py:112
  339.3 6.8 fusion.233
  347.5 6.3 fusion.48
  361.2 26.1 %psum.122 = f32[128,64]{0,1:T(8,128)S(1)} all-reduce(f32[128,64]{0,1:T(8,128)S(1)} %broadcast_select_fusion.2), channel_id=1, replica_groups=mesh['rows'=4,'cols'=8] {'cols'}, use_global_device_ids=true, to_apply=%region_20.21 | all-reduce | flops 8192 | bytes 65536 | tf_op jit(solution)/shard_map/psum | solution.py:112
  387.3 17.2 %psum.123 = f32[128,64]{0,1:T(8,128)S(1)} all-reduce(f32[128,64]{0,1:T(8,128)S(1)} %psum.122), channel_id=1, replica_groups=mesh['rows'=4,'cols'=8] {'rows'}, use_global_device_ids=true, to_apply=%region_21.22 | all-reduce | flops 8192 | bytes 65536 | tf_op jit(solution)/shard_map/psum | solution.py:112
  404.6 6.8 fusion.230
  412.7 6.3 fusion.51
  426.7 26.1 %psum.124 = f32[128,64]{0,1:T(8,128)S(1)} all-reduce(f32[128,64]{0,1:T(8,128)S(1)} %broadcast_select_fusion.1), channel_id=1, replica_groups=mesh['rows'=4,'cols'=8] {'cols'}, use_global_device_ids=true, to_apply=%region_24.25 | all-reduce | flops 8192 | bytes 65536 | tf_op jit(solution)/shard_map/psum | solution.py:112
  452.8 17.2 %psum.125 = f32[128,64]{0,1:T(8,128)S(1)} all-reduce(f32[128,64]{0,1:T(8,128)S(1)} %psum.124), channel_id=1, replica_groups=mesh['rows'=4,'cols'=8] {'rows'}, use_global_device_ids=true, to_apply=%region_25.26 | all-reduce | flops 8192 | bytes 65536 | tf_op jit(solution)/shard_map/psum | solution.py:112
  470.1 6.8 fusion.227
  478.3 4.9 fusion.54
  489.5 26.1 %psum.126 = f32[128,64]{0,1:T(8,128)S(1)} all-reduce(f32[128,64]{0,1:T(8,128)S(1)} %broadcast_select_fusion), channel_id=1, replica_groups=mesh['rows'=4,'cols'=8] {'cols'}, use_global_device_ids=true, to_apply=%region_28.29 | all-reduce | flops 8192 | bytes 65536 | tf_op jit(solution)/shard_map/psum | solution.py:112
  515.6 17.2 %psum.127 = f32[128,64]{0,1:T(8,128)S(1)} all-reduce(f32[128,64]{0,1:T(8,128)S(1)} %psum.126), channel_id=1, replica_groups=mesh['rows'=4,'cols'=8] {'rows'}, use_global_device_ids=true, to_apply=%region_29.30 | all-reduce | flops 8192 | bytes 65536 | tf_op jit(solution)/shard_map/psum | solution.py:112
  532.9 6.8 fusion.224
  541.1 4.9 fusion.57
  574.6 5.2 fusion.409
  579.8 4.6 reshape.2901
  584.4 4.6 reshape.2900
  589.0 4.6 reshape.2905
  593.6 4.6 reshape.2904
  598.2 4.7 reshape.2903
  602.8 4.6 reshape.2902
  610.0 10.3 %fusion.10 = f32[8,16,64,64]{3,2,1,0:T(8,128)S(1)} fusion(f32[16,70,8,64]{3,2,1,0:T(8,128)} %reshape.2901, f32[8,64,70,1]{2,0,1,3:T(8,128)} %get-tuple-element.61), kind=kOutput, calls=%fused_computation.18 | convolution fusion | flops 440401920 | bytes 4534272 | tf_op jit(solution)/shard_map/txi,yitm->yxtm/dot_general | solution.py:132
  620.4 12.1 %fusion.12 = f32[8,16,64,64]{3,2,1,0:T(8,128)} fusion(f32[16,70,8,64]{3,2,1,0:T(8,128)} %reshape.2900, f32[8,64,70,1]{2,0,1,3:T(8,128)S(1)} %copy-done.17), kind=kOutput, calls=%fused_computation.20 | convolution fusion | flops 440401920 | bytes 4534272 | tf_op jit(solution)/shard_map/txi,yitm->yxtm/dot_general | solution.py:132
  632.5 9.4 %fusion.2 = f32[8,16,64,64]{3,2,1,0:T(8,128)} fusion(f32[16,70,8,64]{3,2,1,0:T(8,128)S(1)} %bitcast.856, f32[8,64,70,1]{2,0,1,3:T(8,128)S(1)} %copy-done.16), kind=kOutput, calls=%fused_computation.10 | convolution fusion | flops 440401920 | bytes 4534272 | tf_op jit(solution)/shard_map/txi,yitm->yxtm/dot_general | solution.py:132
  641.9 9.6 %fusion.4 = f32[8,16,64,64]{3,2,1,0:T(8,128)} fusion(f32[16,70,8,64]{3,2,1,0:T(8,128)S(1)} %bitcast.854, f32[8,64,70,1]{2,0,1,3:T(8,128)S(1)} %copy-done.15), kind=kOutput, calls=%fused_computation.12 | convolution fusion | flops 440401920 | bytes 4534272 | tf_op jit(solution)/shard_map/txi,yitm->yxtm/dot_general | solution.py:132
  651.6 9.5 %fusion.6 = f32[8,16,64,64]{3,2,1,0:T(8,128)} fusion(f32[16,70,8,64]{3,2,1,0:T(8,128)S(1)} %bitcast.852, f32[8,64,70,1]{2,0,1,3:T(8,128)S(1)} %copy-done.14), kind=kOutput, calls=%fused_computation.14 | convolution fusion | flops 440401920 | bytes 4534272 | tf_op jit(solution)/shard_map/txi,yitm->yxtm/dot_general | solution.py:132
  661.1 9.4 %fusion.8 = f32[8,16,64,64]{3,2,1,0:T(8,128)} fusion(f32[16,70,8,64]{3,2,1,0:T(8,128)S(1)} %bitcast.850, f32[8,64,70,1]{2,0,1,3:T(8,128)S(1)} %get-tuple-element.60), kind=kOutput, calls=%fused_computation.16 | convolution fusion | flops 440401920 | bytes 4534272 | tf_op jit(solution)/shard_map/txi,yitm->yxtm/dot_general | solution.py:132
  670.6 13.5 %add_bitcast_fusion = f32[16,64,8,64]{1,3,0,2:T(8,128)} fusion(f32[8,16,64,64]{3,2,1,0:T(8,128)S(1)} %copy-done.10, f32[8,16,64,64]{3,2,1,0:T(8,128)} %fusion.4, f32[8,16,64,64]{3,2,1,0:T(8,128)} %fusion.6, f32[8,16,64,64]{3,2,1,0:T(8,128)} %fusion.8, f32[8,16,64,64]{3,2,1,0:T(8,128)S(1)} %copy-done.9, f32[8,16,64,64]{3,2,1,0:T(8,128)S(1)} %fusion.10, ...), kind=kOutput, calls=%fused_computation.24 | convolution fusion | flops 443547648 | bytes 17117184 | tf_op jit(solution)/shard_map/txi,yitm->yxtm/dot_general | solution.py:132
  684.1 5.4 copy.99
  689.5 7.8 %convolution_bitcast_fusion = f32[16,64,8,64]{3,2,1,0:T(8,128)} fusion(f32[16,64,8,64]{3,2,1,0:T(8,128)} %copy.99, f32[8,8]{1,0:T(8,128)S(1)} %copy-done.45), kind=kOutput, calls=%fused_computation.40 | convolution fusion | flops 50331648 | bytes 4194560 | tf_op jit(solution)/shard_map/st,yxtm->yxsm/dot_general | solution.py:138
  697.3 4.8 reshape.2792
  (298 shorter events, 110.8 us)
Async XLA Ops:
  0.0 562.5 %copy-start = (f32[8,7,7]{2,0,1:T(8,128)S(1)}, f32[8,7,7]{2,0,1:T(8,128)}, u32[]{:S(2)}) copy-start(f32[8,7,7]{2,0,1:T(8,128)} %param.16) | copy-start | bytes 4708
  0.0 24.3 %copy-start.13 = (f32[16,64,512]{2,1,0:T(8,128)S(1)}, f32[16,64,512]{2,1,0:T(8,128)}, u32[]{:S(2)}) copy-start(f32[16,64,512]{2,1,0:T(8,128)} %param.9) | copy-start | bytes 6291460
  29.5 58.3 %copy-start.8 = (f32[1024,8,64]{0,2,1:T(8,128)}, f32[1024,8,64]{0,2,1:T(8,128)S(1)}, u32[]{:S(2)}) copy-start(f32[1024,8,64]{0,2,1:T(8,128)S(1)} %copy.67) | copy-start | bytes 6291460
  93.1 49.6 %copy-start.46 = (f32[8,128]{1,0:T(8,128)S(1)}, f32[8,128]{1,0:T(8,128)}, u32[]{:S(2)}) copy-start(f32[8,128]{1,0:T(8,128)} %param.12) | copy-start | bytes 12292
  96.0 53.6 %copy-start.47 = (f32[8,128]{1,0:T(8,128)S(1)}, f32[8,128]{1,0:T(8,128)}, u32[]{:S(2)}) copy-start(f32[8,128]{1,0:T(8,128)} %param.13) | copy-start | bytes 12292
  96.0 54.2 %copy-start.22 = (f32[16,128]{1,0:T(8,128)S(1)}, f32[16,128]{1,0:T(8,128)}, u32[]{:S(2)}) copy-start(f32[16,128]{1,0:T(8,128)} %get-tuple-element.135) | copy-start | bytes 24580
  157.2 7.7 %copy-start.41 = (s32[128]{0:T(128)S(1)}, s32[128]{0:T(128)}, u32[]{:S(2)}) copy-start(s32[128]{0:T(128)} %copy-done.40) | copy-start | bytes 1540
  157.2 7.7 %copy-start.53 = (s32[128]{0:T(128)S(1)}, s32[128]{0:T(128)}, u32[]{:S(2)}) copy-start(s32[128]{0:T(128)} %get-tuple-element.107) | copy-start | bytes 1540
  157.2 51.1 %copy-start.2 = (f32[1024,8,64]{0,2,1:T(8,128)S(1)}, f32[1024,8,64]{0,2,1:T(8,128)}, u32[]{:S(2)}) copy-start(f32[1024,8,64]{0,2,1:T(8,128)} %fusion.39) | copy-start | bytes 6291460
  161.8 53.9 %copy-start.21 = (f32[16,128]{1,0:T(8,128)S(1)}, f32[16,128]{1,0:T(8,128)}, u32[]{:S(2)}) copy-start(f32[16,128]{1,0:T(8,128)} %get-tuple-element.136) | copy-start | bytes 24580
  222.8 7.4 %copy-start.39 = (s32[128]{0:T(128)S(1)}, s32[128]{0:T(128)}, u32[]{:S(2)}) copy-start(s32[128]{0:T(128)} %copy-done.38) | copy-start | bytes 1540
  222.8 7.4 %copy-start.52 = (s32[128]{0:T(128)S(1)}, s32[128]{0:T(128)}, u32[]{:S(2)}) copy-start(s32[128]{0:T(128)} %get-tuple-element.104) | copy-start | bytes 1540
  222.8 50.8 %copy-start.3 = (f32[1024,8,64]{0,2,1:T(8,128)S(1)}, f32[1024,8,64]{0,2,1:T(8,128)}, u32[]{:S(2)}) copy-start(f32[1024,8,64]{0,2,1:T(8,128)} %fusion.42) | copy-start | bytes 6291460
  227.0 54.1 %copy-start.20 = (f32[16,128]{1,0:T(8,128)S(1)}, f32[16,128]{1,0:T(8,128)}, u32[]{:S(2)}) copy-start(f32[16,128]{1,0:T(8,128)} %get-tuple-element.137) | copy-start | bytes 24580
  288.1 7.7 %copy-start.37 = (s32[128]{0:T(128)S(1)}, s32[128]{0:T(128)}, u32[]{:S(2)}) copy-start(s32[128]{0:T(128)} %copy-done.36) | copy-start | bytes 1540
  288.1 7.7 %copy-start.51 = (s32[128]{0:T(128)S(1)}, s32[128]{0:T(128)}, u32[]{:S(2)}) copy-start(s32[128]{0:T(128)} %get-tuple-element.122) | copy-start | bytes 1540
  288.1 51.1 %copy-start.4 = (f32[1024,8,64]{0,2,1:T(8,128)S(1)}, f32[1024,8,64]{0,2,1:T(8,128)}, u32[]{:S(2)}) copy-start(f32[1024,8,64]{0,2,1:T(8,128)} %fusion.45) | copy-start | bytes 6291460
  292.7 54.0 %copy-start.19 = (f32[16,128]{1,0:T(8,128)S(1)}, f32[16,128]{1,0:T(8,128)}, u32[]{:S(2)}) copy-start(f32[16,128]{1,0:T(8,128)} %get-tuple-element.138) | copy-start | bytes 24580
  353.8 7.4 %copy-start.35 = (s32[128]{0:T(128)S(1)}, s32[128]{0:T(128)}, u32[]{:S(2)}) copy-start(s32[128]{0:T(128)} %copy-done.34) | copy-start | bytes 1540
  353.8 7.4 %copy-start.50 = (s32[128]{0:T(128)S(1)}, s32[128]{0:T(128)}, u32[]{:S(2)}) copy-start(s32[128]{0:T(128)} %get-tuple-element.119) | copy-start | bytes 1540
  353.8 50.8 %copy-start.5 = (f32[1024,8,64]{0,2,1:T(8,128)S(1)}, f32[1024,8,64]{0,2,1:T(8,128)}, u32[]{:S(2)}) copy-start(f32[1024,8,64]{0,2,1:T(8,128)} %fusion.48) | copy-start | bytes 6291460
  358.0 53.9 %copy-start.18 = (f32[16,128]{1,0:T(8,128)S(1)}, f32[16,128]{1,0:T(8,128)}, u32[]{:S(2)}) copy-start(f32[16,128]{1,0:T(8,128)} %get-tuple-element.139) | copy-start | bytes 24580
  419.0 7.7 %copy-start.33 = (s32[128]{0:T(128)S(1)}, s32[128]{0:T(128)}, u32[]{:S(2)}) copy-start(s32[128]{0:T(128)} %copy-done.32) | copy-start | bytes 1540
  419.0 7.7 %copy-start.49 = (s32[128]{0:T(128)S(1)}, s32[128]{0:T(128)}, u32[]{:S(2)}) copy-start(s32[128]{0:T(128)} %get-tuple-element.116) | copy-start | bytes 1540
  419.0 51.1 %copy-start.6 = (f32[1024,8,64]{0,2,1:T(8,128)S(1)}, f32[1024,8,64]{0,2,1:T(8,128)}, u32[]{:S(2)}) copy-start(f32[1024,8,64]{0,2,1:T(8,128)} %fusion.51) | copy-start | bytes 6291460
  470.1 8.2 %copy-start.7 = (f32[1024,8,64]{0,2,1:T(8,128)S(1)}, f32[1024,8,64]{0,2,1:T(8,128)}, u32[]{:S(2)}) copy-start(f32[1024,8,64]{0,2,1:T(8,128)} %fusion.51) | copy-start | bytes 6291460
  548.4 8.8 %copy-start.12 = (f32[1024,8,64]{0,2,1:T(8,128)S(1)}, f32[1024,8,64]{0,2,1:T(8,128)}, u32[]{:S(2)}) copy-start(f32[1024,8,64]{0,2,1:T(8,128)} %copy-done.11) | copy-start | bytes 6291460
  550.8 12.5 %collective-permute-start = (f32[3,64,512]{2,1,0:T(8,128)}, f32[3,64,512]{2,1,0:T(8,128)}, u32[]{:S(2)}, u32[]{:S(2)}) collective-permute-start(f32[3,64,512]{2,1,0:T(8,128)} %slice.114), channel_id=1, source_target_pairs={{0,8},{8,16},{16,24},{1,9},{9,17},{17,25},{2,10},{10,18},{18,26},{... | collective-permute-start | bytes 1179656 | tf_op jit(solution)/shard_map/ppermute | solution.py:18
  555.2 9.1 %collective-permute-start.1 = (f32[3,64,512]{2,1,0:T(8,128)S(1)}, f32[3,64,512]{2,1,0:T(8,128)S(1)}, u32[]{:S(2)}, u32[]{:S(2)}) collective-permute-start(f32[3,64,512]{2,1,0:T(8,128)S(1)} %slice.116), channel_id=1, source_target_pairs={{8,0},{16,8},{24,16},{9,1},{17,9},{25,17},{10,2},{18,10},{26,18},{... | collective-permute-start | bytes 1179656 | tf_op jit(solution)/shard_map/ppermute | solution.py:19
  565.2 3.9 collective-permute-start.2
  566.5 6.7 collective-permute-start.3
  607.4 25.0 %slice-start.6 = ((s8[4587520]{0:T(1024)(128)(4,1)}), s8[393216]{0:T(1024)(128)(4,1)S(1)}, s32[]{:S(2)}) async-start(s8[4587520]{0:T(1024)(128)(4,1)} %bitcast.855), calls=%async_computation.6 | async-start | bytes 786432
  610.0 10.3 %copy-start.17 = (f32[8,64,70,1]{2,0,1,3:T(8,128)S(1)}, f32[8,64,70,1]{2,0,1,3:T(8,128)}, u32[]{:S(2)}) copy-start(f32[8,64,70,1]{2,0,1,3:T(8,128)} %get-tuple-element.62) | copy-start | bytes 430084
  610.0 22.4 %slice-start.7 = ((s8[4587520]{0:T(1024)(128)(4,1)}), s8[4194304]{0:T(1024)(128)(4,1)S(1)}, s32[]{:S(2)}) async-start(s8[4587520]{0:T(1024)(128)(4,1)} %bitcast.855), calls=%async_computation.7 | async-start | bytes 8388608
  620.3 12.1 %copy-start.16 = (f32[8,64,70,1]{2,0,1,3:T(8,128)S(1)}, f32[8,64,70,1]{2,0,1,3:T(8,128)}, u32[]{:S(2)}) copy-start(f32[8,64,70,1]{2,0,1,3:T(8,128)} %get-tuple-element.57) | copy-start | bytes 430084
  620.4 21.5 %slice-start.4 = ((s8[4587520]{0:T(1024)(128)(4,1)}), s8[4194304]{0:T(1024)(128)(4,1)S(1)}, s32[]{:S(2)}) async-start(s8[4587520]{0:T(1024)(128)(4,1)} %bitcast.853), calls=%async_computation.4 | async-start | bytes 8388608
  620.4 31.2 %slice-start.2 = ((s8[4587520]{0:T(1024)(128)(4,1)}), s8[4194304]{0:T(1024)(128)(4,1)S(1)}, s32[]{:S(2)}) async-start(s8[4587520]{0:T(1024)(128)(4,1)} %bitcast.851), calls=%async_computation.2 | async-start | bytes 8388608
  632.5 9.4 %slice-start.5 = ((s8[4587520]{0:T(1024)(128)(4,1)}), s8[393216]{0:T(1024)(128)(4,1)S(1)}, s32[]{:S(2)}) async-start(s8[4587520]{0:T(1024)(128)(4,1)} %bitcast.853), calls=%async_computation.5 | async-start | bytes 786432
  632.5 9.4 %copy-start.15 = (f32[8,64,70,1]{2,0,1,3:T(8,128)S(1)}, f32[8,64,70,1]{2,0,1,3:T(8,128)}, u32[]{:S(2)}) copy-start(f32[8,64,70,1]{2,0,1,3:T(8,128)} %get-tuple-element.58) | copy-start | bytes 430084
  632.5 19.1 %slice-start.3 = ((s8[4587520]{0:T(1024)(128)(4,1)}), s8[393216]{0:T(1024)(128)(4,1)S(1)}, s32[]{:S(2)}) async-start(s8[4587520]{0:T(1024)(128)(4,1)} %bitcast.851), calls=%async_computation.3 | async-start | bytes 786432
  641.9 9.7 %copy-start.14 = (f32[8,64,70,1]{2,0,1,3:T(8,128)S(1)}, f32[8,64,70,1]{2,0,1,3:T(8,128)}, u32[]{:S(2)}) copy-start(f32[8,64,70,1]{2,0,1,3:T(8,128)} %get-tuple-element.59) | copy-start | bytes 430084
  641.9 19.2 %slice-start = ((s8[4587520]{0:T(1024)(128)(4,1)}), s8[4194304]{0:T(1024)(128)(4,1)S(1)}, s32[]{:S(2)}) async-start(s8[4587520]{0:T(1024)(128)(4,1)} %bitcast.849), calls=%async_computation | async-start | bytes 8388608
  651.6 9.5 %slice-start.1 = ((s8[4587520]{0:T(1024)(128)(4,1)}), s8[393216]{0:T(1024)(128)(4,1)S(1)}, s32[]{:S(2)}) async-start(s8[4587520]{0:T(1024)(128)(4,1)} %bitcast.849), calls=%async_computation.1 | async-start | bytes 786432
  651.6 18.9 %slice-start.8 = ((s8[4587520]{0:T(1024)(128)(4,1)}), s8[4194304]{0:T(1024)(128)(4,1)S(1)}, s32[]{:S(2)}) async-start(s8[4587520]{0:T(1024)(128)(4,1)} %bitcast.857), calls=%async_computation.8 | async-start | bytes 8388608
  661.1 9.4 %slice-start.9 = ((s8[4587520]{0:T(1024)(128)(4,1)}), s8[393216]{0:T(1024)(128)(4,1)S(1)}, s32[]{:S(2)}) async-start(s8[4587520]{0:T(1024)(128)(4,1)} %bitcast.857), calls=%async_computation.9 | async-start | bytes 786432
  661.1 9.4 %copy-start.9 = (f32[8,16,64,64]{3,2,1,0:T(8,128)S(1)}, f32[8,16,64,64]{3,2,1,0:T(8,128)}, u32[]{:S(2)}) copy-start(f32[8,16,64,64]{3,2,1,0:T(8,128)} %fusion.12) | copy-start | bytes 6291460
  661.1 9.4 %copy-start.10 = (f32[8,16,64,64]{3,2,1,0:T(8,128)S(1)}, f32[8,16,64,64]{3,2,1,0:T(8,128)}, u32[]{:S(2)}) copy-start(f32[8,16,64,64]{3,2,1,0:T(8,128)} %fusion.2) | copy-start | bytes 6291460
  689.5 12.6 %copy-start.1 = (f32[8,7,7]{2,0,1:T(8,128)S(1)}, f32[8,7,7]{2,0,1:T(8,128)}, u32[]{:S(2)}) copy-start(f32[8,7,7]{2,0,1:T(8,128)} %param.16) | copy-start | bytes 4708
  (28 other events, 122.1 us)
